TPU v7x, 128 devices: a whole 4x4x4 slice. The times are simulated.
128 devices in a mesh: atom: 16 (over y, x), mode: 8 (over z, core).
Axes of the slice: x: 4, y: 4, z: 4, core: 2. Of those that a mesh axis runs over, the one named last changes fastest.
Arguments:
- eigvec: bfloat16 [3, 4096, 2048], P(None, 'atom', 'mode'), may hold values from -0.0546875 to 0.0546875
- force: float32 [3, 3, 16, 4096], P(None, None, None, 'atom'), may hold values from -12 to 12
- bond: float32 [3, 16, 4096], P(None, None, 'atom'), may hold values from -6 to 6
- nbr: int32 [16, 4096], P(None, 'atom'), may hold values from 0 to 4095, as said below
- band: int32 [2, 2048], P(None, 'mode'), may hold values from 0 to 2048, as said below
- freq: float32 [2048], P('mode'), may hold values from 0.5 to 4, as said below
Outputs:
- diffusivity: float32 [2048], P('mode')
- conductivity: float32 [2048], P('mode')
Inputs may be any that keep to these rules, and one draw needn't show every extreme that they name: `nbr`: each entry is an atom whose position in atom order differs from that of its own atom by 1 to 128, counted cyclically over the 4096 atoms; the distance 128 occurs in every draw. For every mode i: max(0, i - 128) <= band[0, i] <= i < band[1, i] <= min(2048, i + 129); both outer limits are reached at some mode. `freq`: strictly increasing along the modes.
All inputs are finite; a program needn't handle non-finite values.
Results may differ from a plain program's by a relative error of at most 0.00057.
Values may be sent and summed in bfloat16 or wider, within the bound.
A program may use at most 64 MiB of HBM per device.

v0:
```python
import math
import jax
import jax.numpy as jnp
from jax import lax
from jax.sharding import PartitionSpec as P

ATOM_DEV = 256
MODE_DEV = 256
RIM = 128
HALF = 128
BROAD = 128


def extended(shard, sides, width, wrap):
    for axis, dim in sides:
        size, length = (lax.axis_size(axis), shard.shape[dim])
        up = [(i, (i + 1) % size) for i in range(size if wrap else size - 1)]
        down = [(j, i) for i, j in up]
        last = lax.slice_in_dim(shard, length - width, length, axis=dim)
        first = lax.slice_in_dim(shard, 0, width, axis=dim)
        before = lax.ppermute(last, axis, up)
        after = lax.ppermute(first, axis, down)
        shard = jnp.concatenate([before, shard, after], axis=dim)
    return shard


def prefix(part, axis, combine, identity):
    place = lax.axis_index(axis)
    gathered = lax.all_gather(part, axis)
    state = jnp.zeros_like(part) + jnp.asarray(identity, part.dtype)

    def one(lap, state):
        return combine(state, lax.dynamic_index_in_dim(gathered, lap, 0, False))

    return lax.fori_loop(0, place, one, state)


def capacity_of(spectral):
    return spectral * spectral * jnp.exp(spectral) / jnp.expm1(spectral) ** 2


def pair_weight(own_freq, partner_freq, own_ids, partner_ids, lower_end, upper_end, broaden):
    inside = (
        (partner_ids[:, None] >= lower_end[None, :])
        & (partner_ids[:, None] < upper_end[None, :])
        & (partner_ids[:, None] != own_ids[None, :])
    )
    detune = own_freq[None, :] - partner_freq[:, None]
    lorentz = broaden / math.pi / (detune * detune + broaden * broaden)
    factor = (own_freq[None, :] + partner_freq[:, None]) ** 2 / (
        4.0 * own_freq[None, :] * partner_freq[:, None]
    )
    return jnp.where(inside, lorentz * factor, 0.0)


def add_totals(earlier, later):
    return earlier + later


def body(eigvec, force, bond, nbr, band, freq):
    atom_count = ATOM_DEV * lax.axis_size("atom")
    mode_count = MODE_DEV * lax.axis_size("mode")
    partner_span = MODE_DEV + 2 * HALF
    spectrum = lax.all_gather(freq, "mode", axis=0, tiled=True)
    atom_rows = extended(eigvec, (("atom", 1),), RIM, True)
    band_rows = extended(eigvec, (("mode", 2),), HALF, False)
    row_major = jnp.transpose(atom_rows, (1, 0, 2))
    domain = lax.axis_index("atom")
    local_ids = (nbr - domain * ATOM_DEV + RIM + atom_count) % atom_count
    block_size = min(512, ATOM_DEV)
    gathered = jnp.take(row_major, local_ids, axis=0)
    coupling = (bond[:, None, None, :, 0:block_size] * force[None, :, :, :, 0:block_size]).astype(
        jnp.bfloat16
    )
    block_image = jnp.einsum(
        "kcdna,nadi->kcai", coupling, gathered, preferred_element_type=jnp.float32
    )
    pieces = block_image.astype(jnp.bfloat16)
    pair_terms = jnp.einsum("caj,kcai->kji", band_rows, pieces, preferred_element_type=jnp.float32)
    mode_block = lax.axis_index("mode")
    mode_start = mode_block * MODE_DEV
    broaden = BROAD * (jnp.max(spectrum) - jnp.min(spectrum)) / (mode_count - 1)
    padded_freq = jnp.pad(spectrum, (HALF, HALF), constant_values=1.0)
    partner_freq = lax.dynamic_slice_in_dim(padded_freq, mode_start, partner_span)
    partner_ids = mode_start - HALF + jnp.arange(partner_span, dtype=jnp.int32)
    own_ids = mode_start + jnp.arange(MODE_DEV, dtype=jnp.int32)
    weight = pair_weight(freq, partner_freq, own_ids, partner_ids, band[0], band[1], broaden)
    summed_pair = lax.psum(pair_terms, "atom")
    strength = jnp.sum(summed_pair * summed_pair, axis=0)
    row_sums = jnp.sum(weight * strength, axis=0)
    diffusivity = math.pi / (3.0 * freq * freq) * row_sums
    running = jnp.cumsum(capacity_of(freq) * diffusivity)
    device_total = running[-1]
    earlier_sum = prefix(device_total, "mode", add_totals, jnp.float32(0.0))
    conductivity = (earlier_sum + running) / MODE_DEV
    return (diffusivity, conductivity)


def solution(mesh):
    in_specs = (
        P(None, "atom", "mode"),
        P(None, None, None, "atom"),
        P(None, None, "atom"),
        P(None, "atom"),
        P(None, "mode"),
        P("mode"),
    )
    out_specs = (P("mode"), P("mode"))
    return jax.shard_map(body, mesh=mesh, in_specs=in_specs, out_specs=out_specs, check_vma=False)
```

profile of v0, /device:TPU:97, one launch (start us, length us, event | category | flops | bytes accessed | tf_op | source)
XLA Modules:
  0.0 190.9 jit_solution(17926169755393144528)
XLA Ops:
  7.2 0.0 copy-start
  7.2 0.0 copy-start.3
  7.2 0.0 copy-start.2
  7.2 0.0 all-reduce.4.cloned.1.call-start
  7.2 1.4 copy.12
  8.6 0.0 copy-start.4
  8.6 0.2 fusion.21
  8.8 5.0 %collective-permute-start.1 = (bf16[3,128,256]{2,0,1:T(4,128)(2,1)S(1)}, bf16[3,128,256]{2,0,1:T(4,128)(2,1)}, u32[]{:S(2)}, u32[]{:S(2)}) collective-permute-start(bf16[3,128,256]{2,0,1:T(4,128)(2,1)S(1)} %get-tuple-element.39), channel_id=1, source_target_pairs={{8,0},{16,8},{24,16},{32,24},{40,32},{48,40},{56,48},{64,56},{72,6... | collective-permute-start | bytes 589832 | tf_op jit(solution)/shard_map/ppermute | solution.py:22
  13.8 0.0 collective-permute-start
  13.8 0.8 fusion.22
  14.7 3.5 %collective-permute-start.3 = (bf16[3,256,128]{2,1,0:T(8,128)(2,1)}, bf16[3,256,128]{2,1,0:T(8,128)(2,1)}, u32[]{:S(2)}, u32[]{:S(2)}) collective-permute-start(bf16[3,256,128]{2,1,0:T(8,128)(2,1)} %get-tuple-element.41), channel_id=1, source_target_pairs={{1,0},{2,1},{3,2},{4,3},{5,4},{6,5},{7,6},{9,8},{10,9},{11,10},{12... | collective-permute-start | bytes 589832 | tf_op jit(solution)/shard_map/ppermute | solution.py:22
  18.2 1.3 collective-permute-start.2
  19.6 0.7 copy.17
  20.3 1.1 copy.16
  21.4 0.7 copy.11
  22.1 0.0 collective-permute-done.1
  22.1 2.1 %collective-permute-done = bf16[3,128,256]{2,0,1:T(4,128)(2,1)} collective-permute-done((bf16[3,128,256]{2,0,1:T(4,128)(2,1)S(1)}, bf16[3,128,256]{2,0,1:T(4,128)(2,1)}, u32[]{:S(2)}, u32[]{:S(2)}) %collective-permute-start) | collective-permute-done | bytes 196640 | tf_op jit(solution)/shard_map/ppermute | solution.py:21
  24.2 1.8 maximum_bitcast_fusion
  25.9 32.8 %gather_fusion = bf16[4096,3,256]{2,1,0:T(4,128)(2,1)} fusion(bf16[512,3,256]{2,1,0:T(4,128)(2,1)S(1)} %maximum_bitcast_fusion, s32[4096]{0:T(1024)S(1)} %broadcast_clamp_fusion), kind=kCustom, calls=%fused_computation | custom fusion | bytes 12599296 | tf_op jit(solution)/shard_map/jit(_take)/gather | solution.py:71
  58.7 9.2 %fusion.8 = bf16[3,3,256,256]{3,1,0,2:T(4,128)(2,1)S(1)} fusion(f32[3,3,16,256]{2,0,1,3:T(4,128)S(1)} %copy.17, f32[3,16,256]{1,0,2:T(4,128)S(1)} %copy-done.1, bf16[16,256,3,256]{3,2,1,0:T(4,128)(2,1)} %bitcast.42, pred[16,256]{0,1:T(8,128)(4,1)} %copy.11), kind=kOutput, calls=%fused_computation.11 | convolution fusion | flops 60579840 | bytes 7671808 | tf_op jit(solution)/shard_map/kcdna,nadi->kcai/dot_general | solution.py:75
  67.9 0.0 collective-permute-done.3
  67.9 0.0 collective-permute-done.2
  68.0 3.0 %convolution_bitcast_fusion = f32[3,512,256]{1,2,0:T(8,128)} fusion(bf16[3,3,256,256]{3,1,0,2:T(4,128)(2,1)S(1)} %fusion.8, bf16[3,256,128]{2,1,0:T(8,128)(2,1)} %collective-permute-done.3, bf16[3,256,256]{2,1,0:T(8,128)(2,1)S(1)} %copy-done, bf16[3,256,128]{2,1,0:T(8,128)(2,1)} %collective-permute-done.2), kind=kOutput, calls=%fused_computation.12 | convolution fusion | flops 606339072 | bytes 3538944 | tf_op jit(solution)/shard_map/caj,kcai->kji/dot_general | solution.py:79
  71.0 0.0 all-reduce.4.cloned.1.call-update
  71.0 0.6 copy-done.5
  71.6 8.7 %all-gather = f32[8,1,256]{2,1,0:T(1,128)S(1)} all-gather(f32[1,1,256]{2,1,0:T(1,128)S(1)} %bitcast.45), channel_id=1, replica_groups=mesh['atom'=16,'mode'=8] {'mode'}, dimensions={0}, use_global_device_ids=true | all-gather | bytes 9216 | tf_op jit(solution)/shard_map/all_gather | solution.py:64
  80.3 0.6 fusion.20
  82.3 0.6 dynamic-slice
  82.9 0.1 pad_dynamic-slice_fusion
  83.0 74.9 %all-reduce.4.cloned.1.call-done = f32[3,512,256]{1,2,0:T(8,128)} async-done(((f32[3,512,256]{1,2,0:T(8,128)}), f32[3,512,256]{1,2,0:T(8,128)}) %all-reduce.4.cloned.1.call-update) | async-done | bytes 1572880 | tf_op jit(solution)/shard_map/psum | solution.py:88
  157.8 1.6 multiply_reduce_fusion
  159.5 0.5 multiply_reduce_fusion.1
  160.0 0.6 multiply_bitcast_fusion
  160.6 0.3 reduce-window.9
  160.9 0.1 slice.34
  161.0 0.1 slice_reduce_fusion
  161.1 0.1 add_bitcast_fusion
  161.2 0.8 slice_dynamic-update-slice_fusion
  162.0 11.9 %all-reduce.1 = f32[8]{0:T(128)S(1)} all-reduce(f32[8]{0:T(128)S(1)} %slice_dynamic-update-slice_fusion), channel_id=1, replica_groups=mesh['atom'=16,'mode'=8] {'mode'}, use_global_device_ids=true, to_apply=%add.1 | all-reduce | flops 8 | bytes 64
  173.8 9.7 %while.10 = (s32[]{:T(128)}, f32[]{:T(128)}, s32[]{:T(128)}, f32[8]{0:T(128)S(1)}, s32[]{:T(128)}, /*index=5*/s32[]{:T(128)}, s32[]{:T(128)}) while((s32[]{:T(128)}, f32[]{:T(128)}, s32[]{:T(128)}, f32[8]{0:T(128)S(1)}, s32[]{:T(128)}, /*index=5*/s32[]{:T(128)}, s32[]{:T(128)}) %tuple.27), condition=%wide.region_8.9_spmd, body=%wide.region_7.8_spmd.sunk | while | flops 6 | bytes 143 | solution.py:35
  173.8 0.7 dynamic_slice.10
  175.2 0.7 dynamic_slice.10
  176.6 0.7 dynamic_slice.10
  178.0 0.7 dynamic_slice.10
  179.4 0.7 dynamic_slice.10
  180.8 0.7 dynamic_slice.10
  182.1 0.7 dynamic_slice.10
  183.5 0.6 add_multiply_fusion
  (21 shorter events, 0.1 us)
Async XLA Ops:
  7.2 6.7 %copy-start = (bf16[3,256,256]{2,1,0:T(8,128)(2,1)S(1)}, bf16[3,256,256]{2,1,0:T(8,128)(2,1)}, u32[]{:S(2)}) copy-start(bf16[3,256,256]{2,1,0:T(8,128)(2,1)} %param.8) | copy-start | bytes 1179652
  7.2 12.3 %copy-start.3 = (s32[16,256]{1,0:T(8,128)S(1)}, s32[16,256]{1,0:T(8,128)}, u32[]{:S(2)}) copy-start(s32[16,256]{1,0:T(8,128)} %param.11) | copy-start | bytes 49156
  7.2 12.4 %copy-start.2 = (f32[3,3,16,256]{3,2,1,0:T(8,128)S(1)}, f32[3,3,16,256]{3,2,1,0:T(8,128)}, u32[]{:S(2)}) copy-start(f32[3,3,16,256]{3,2,1,0:T(8,128)} %param.9) | copy-start | bytes 442372
  7.2 150.6 %all-reduce.4.cloned.1.call-start = ((), (), s32[]{:S(2)}) async-start(), calls=%async_computation | async-start | bytes 3145728 | tf_op jit(solution)/shard_map/psum | solution.py:88
  8.6 11.7 %copy-start.4 = (f32[3,16,256]{2,1,0:T(8,128)S(1)}, f32[3,16,256]{2,1,0:T(8,128)}, u32[]{:S(2)}) copy-start(f32[3,16,256]{2,1,0:T(8,128)} %param.10) | copy-start | bytes 147460
  8.8 13.3 %collective-permute-start.1 = (bf16[3,128,256]{2,0,1:T(4,128)(2,1)S(1)}, bf16[3,128,256]{2,0,1:T(4,128)(2,1)}, u32[]{:S(2)}, u32[]{:S(2)}) collective-permute-start(bf16[3,128,256]{2,0,1:T(4,128)(2,1)S(1)} %get-tuple-element.39), channel_id=1, source_target_pairs={{8,0},{16,8},{24,16},{32,24},{40,32},{48,40},{56,48},{64,56},{72,6... | collective-permute-start | bytes 589832 | tf_op jit(solution)/shard_map/ppermute | solution.py:22
  13.8 10.3 %collective-permute-start = (bf16[3,128,256]{2,0,1:T(4,128)(2,1)S(1)}, bf16[3,128,256]{2,0,1:T(4,128)(2,1)}, u32[]{:S(2)}, u32[]{:S(2)}) collective-permute-start(bf16[3,128,256]{2,0,1:T(4,128)(2,1)S(1)} %get-tuple-element.38), channel_id=1, source_target_pairs={{0,8},{8,16},{16,24},{24,32},{32,40},{40,48},{48,56},{56,64},{64,7... | collective-permute-start | bytes 589832 | tf_op jit(solution)/shard_map/ppermute | solution.py:21
  14.7 53.3 %collective-permute-start.3 = (bf16[3,256,128]{2,1,0:T(8,128)(2,1)}, bf16[3,256,128]{2,1,0:T(8,128)(2,1)}, u32[]{:S(2)}, u32[]{:S(2)}) collective-permute-start(bf16[3,256,128]{2,1,0:T(8,128)(2,1)} %get-tuple-element.41), channel_id=1, source_target_pairs={{1,0},{2,1},{3,2},{4,3},{5,4},{6,5},{7,6},{9,8},{10,9},{11,10},{12... | collective-permute-start | bytes 589832 | tf_op jit(solution)/shard_map/ppermute | solution.py:22
  18.2 49.7 %collective-permute-start.2 = (bf16[3,256,128]{2,1,0:T(8,128)(2,1)}, bf16[3,256,128]{2,1,0:T(8,128)(2,1)}, u32[]{:S(2)}, u32[]{:S(2)}) collective-permute-start(bf16[3,256,128]{2,1,0:T(8,128)(2,1)} %get-tuple-element.40), channel_id=1, source_target_pairs={{0,1},{1,2},{2,3},{3,4},{4,5},{5,6},{6,7},{8,9},{9,10},{10,11},{11... | collective-permute-start | bytes 589832 | tf_op jit(solution)/shard_map/ppermute | solution.py:21
  25.9 32.8 %copy-start.1 = (f32[3,16,256]{1,0,2:T(4,128)S(1)}, f32[3,16,256]{1,0,2:T(4,128)}, u32[]{:S(2)}) copy-start(f32[3,16,256]{1,0,2:T(4,128)} %copy.16) | copy-start | bytes 147460
  71.0 0.7 copy-start.5
  71.0 11.3 %copy-start.7 = (u32[128]{0:T(128)S(1)}, u32[128]{0:T(128)}, u32[]{:S(2)}) copy-start(u32[128]{0:T(128)} %constant.93) | copy-start | bytes 1540
  71.0 12.0 %copy-start.6 = (s32[2,256]{1,0:T(2,128)S(1)}, s32[2,256]{1,0:T(2,128)}, u32[]{:S(2)}) copy-start(s32[2,256]{1,0:T(2,128)} %param.12) | copy-start | bytes 6148
Sparse Core Ops, SparseCore 0:
  71.1 86.6 all-reduce.3
where the time goes:
time: 191 us
  waiting for transfers between devices  76.9 us (40%)
  local copies, waits for them, and re-layouts  44.7 us (23%)
  blocking collectives  20.6 us (11%)
  between operations  15.5 us (8%)
  matrix products  12.2 us (6%)
  starting transfers between devices  9.86 us (5%)
  other arithmetic  6.15 us (3%)
  loops' own time  5 us (3%)
    psum x1, waiting for transfers between devices, body(): summed_pair = lax.psum(pair_terms, 'atom')  74.9 us
    gather x1, local copies, waits for them, and re-layouts, body(): gathered = jnp.take(row_major, local_ids, axis=0)  32.8 us
    unnamed x1, blocking collectives  11.9 us
    dot_general x1, matrix products, body(): jnp.einsum('kcdna,nadi->kcai', coupling, gathered, preferred_element_type...  9.23 us
    all_gather x1, blocking collectives, body(): spectrum = lax.all_gather(freq, 'mode', axis=0, tiled=True)  8.7 us
    ppermute x2, starting transfers between devices, extended(): after = lax.ppermute(first, axis, down)  8.54 us
    unnamed x23, local copies, waits for them, and re-layouts  5.23 us
    another operation x1, loops' own time, prefix(): return lax.fori_loop(0, place, one, state)  5 us
  transfers between devices with their start and end apart: 5, of which 2 were waited for; matrix products, arithmetic and copies ran while one was open for 25% of the time, Pallas kernels for 0%

commit v1 on v0

--- a/solution.py
+++ b/solution.py
@@ -85,7 +85,7 @@
     partner_ids = mode_start - HALF + jnp.arange(partner_span, dtype=jnp.int32)
     own_ids = mode_start + jnp.arange(MODE_DEV, dtype=jnp.int32)
     weight = pair_weight(freq, partner_freq, own_ids, partner_ids, band[0], band[1], broaden)
-    summed_pair = lax.psum(pair_terms, "atom")
+    summed_pair = jnp.sum(lax.all_gather(pair_terms, "atom"), axis=0)
     strength = jnp.sum(summed_pair * summed_pair, axis=0)
     row_sums = jnp.sum(weight * strength, axis=0)
     diffusivity = math.pi / (3.0 * freq * freq) * row_sums

time: 191 us -> 267 us (1.40)
  waiting for transfers between devices: 76.9 us -> 144 us
  other arithmetic: 6.15 us -> 14 us
    all_gather x0 -> x1, waiting for transfers between devices: none -> 141 us  [body(): summed_pair = jnp.sum(lax.all_gather(pair_terms, 'atom'), axis=0)]
    psum x1 -> x0, waiting for transfers between devices: 74.9 us -> none  [body(): summed_pair = lax.psum(pair_terms, 'atom')]
    reduce_sum x0 -> x1, other arithmetic: none -> 9.32 us  [body(): summed_pair = jnp.sum(lax.all_gather(pair_terms, 'atom'), axis=0)]
    unnamed x23 -> x24, local copies, waits for them, and re-layouts: 5.23 us -> 5.58 us
  transfers between devices with their start and end apart: 5 -> 5, of which waited for: 2 -> 2; matrix products, arithmetic and copies ran while one was open for 25% -> 18% of each run, Pallas kernels for 0% -> 0%
where the time goes in v1:
time: 267 us; the launch traced here: 266 us
  waiting for transfers between devices  144 us (54%)
  local copies, waits for them, and re-layouts  46.8 us (18%)
  blocking collectives  20.6 us (8%)
  between operations  15.6 us (6%)
  other arithmetic  14 us (5%)
  matrix products  11.1 us (4%)
  starting transfers between devices  9.86 us (4%)
  loops' own time  5 us (2%)
    all_gather x1, waiting for transfers between devices, body(): summed_pair = jnp.sum(lax.all_gather(pair_terms, 'atom'), axis=0)  141 us
    gather x1, local copies, waits for them, and re-layouts, body(): gathered = jnp.take(row_major, local_ids, axis=0)  32.8 us
    unnamed x1, blocking collectives  11.9 us
    reduce_sum x1, other arithmetic, body(): summed_pair = jnp.sum(lax.all_gather(pair_terms, 'atom'), axis=0)  9.32 us
    dot_general x1, matrix products, body(): jnp.einsum('kcdna,nadi->kcai', coupling, gathered, preferred_element_type...  9.23 us
    all_gather x1, blocking collectives, body(): spectrum = lax.all_gather(freq, 'mode', axis=0, tiled=True)  8.7 us
    ppermute x2, starting transfers between devices, extended(): after = lax.ppermute(first, axis, down)  8.54 us
    unnamed x24, local copies, waits for them, and re-layouts  5.58 us
  transfers between devices with their start and end apart: 5, of which 2 were waited for; matrix products, arithmetic and copies ran while one was open for 18% of the time, Pallas kernels for 0%

profile of v1, /device:TPU:97, one launch (start us, length us, event | category | flops | bytes accessed | tf_op | source)
XLA Modules:
  0.0 266.3 jit_solution(3875908340183067456)
XLA Ops:
  7.2 0.0 all-gather.4.cloned.1.call-start
  7.2 1.4 copy.22
  8.6 0.0 copy-start.4
  8.6 0.2 fusion.21
  8.8 5.0 %collective-permute-start.1 = (bf16[3,128,256]{2,0,1:T(4,128)(2,1)S(1)}, bf16[3,128,256]{2,0,1:T(4,128)(2,1)}, u32[]{:S(2)}, u32[]{:S(2)}) collective-permute-start(bf16[3,128,256]{2,0,1:T(4,128)(2,1)S(1)} %get-tuple-element.39), channel_id=1, source_target_pairs={{8,0},{16,8},{24,16},{32,24},{40,32},{48,40},{56,48},{64,56},{72,6... | collective-permute-start | bytes 589832 | tf_op jit(solution)/shard_map/ppermute | solution.py:22
  13.8 0.0 collective-permute-start
  13.8 0.9 fusion.22
  14.7 3.5 %collective-permute-start.3 = (bf16[3,256,128]{2,1,0:T(8,128)(2,1)}, bf16[3,256,128]{2,1,0:T(8,128)(2,1)}, u32[]{:S(2)}, u32[]{:S(2)}) collective-permute-start(bf16[3,256,128]{2,1,0:T(8,128)(2,1)} %get-tuple-element.41), channel_id=1, source_target_pairs={{1,0},{2,1},{3,2},{4,3},{5,4},{6,5},{7,6},{9,8},{10,9},{11,10},{12... | collective-permute-start | bytes 589832 | tf_op jit(solution)/shard_map/ppermute | solution.py:22
  18.2 1.3 collective-permute-start.2
  19.6 0.7 copy.27
  20.4 1.1 copy.26
  21.4 0.7 copy.21
  22.1 0.0 collective-permute-done.1
  22.1 2.0 collective-permute-done
  24.2 1.8 maximum_bitcast_fusion
  25.9 32.8 %gather_fusion = bf16[4096,3,256]{2,1,0:T(4,128)(2,1)} fusion(bf16[512,3,256]{2,1,0:T(4,128)(2,1)S(1)} %maximum_bitcast_fusion, s32[4096]{0:T(1024)S(1)} %broadcast_clamp_fusion), kind=kCustom, calls=%fused_computation | custom fusion | bytes 12599296 | tf_op jit(solution)/shard_map/jit(_take)/gather | solution.py:71
  58.7 9.2 %fusion.8 = bf16[3,3,256,256]{3,1,0,2:T(4,128)(2,1)S(1)} fusion(f32[3,3,16,256]{2,0,1,3:T(4,128)S(1)} %copy.27, f32[3,16,256]{1,0,2:T(4,128)S(1)} %copy-done.1, bf16[16,256,3,256]{3,2,1,0:T(4,128)(2,1)} %bitcast.44, pred[16,256]{0,1:T(8,128)(4,1)} %copy.21), kind=kOutput, calls=%fused_computation.11 | convolution fusion | flops 60579840 | bytes 7671808 | tf_op jit(solution)/shard_map/kcdna,nadi->kcai/dot_general | solution.py:75
  67.9 0.0 collective-permute-done.3
  67.9 0.0 collective-permute-done.2
  68.0 1.8 convolution_bitcast_fusion
  69.8 1.7 copy.29
  71.5 0.0 all-gather.4.cloned.1.call-update
  71.5 0.6 copy-done.5
  72.2 8.7 %all-gather.1 = f32[8,1,256]{2,1,0:T(1,128)S(1)} all-gather(f32[1,1,256]{2,1,0:T(1,128)S(1)} %bitcast.47), channel_id=1, replica_groups=mesh['atom'=16,'mode'=8] {'mode'}, dimensions={0}, use_global_device_ids=true | all-gather | bytes 9216 | tf_op jit(solution)/shard_map/all_gather | solution.py:64
  80.9 0.6 fusion.20
  82.8 0.6 dynamic-slice
  83.4 0.1 pad_dynamic-slice_fusion
  83.5 141.5 %all-gather.4.cloned.1.call-done = f32[48,512,256]{2,1,0:T(8,128)} async-done(((f32[3,512,256]{2,1,0:T(8,128)}), f32[48,512,256]{2,1,0:T(8,128)}) %all-gather.4.cloned.1.call-update) | async-done | bytes 25165840 | tf_op jit(solution)/shard_map/all_gather | solution.py:88
  225.0 9.3 %reduce_sum.27 = f32[3,512,256]{2,1,0:T(8,128)S(1)} reduce(f32[16,3,512,256]{3,2,1,0:T(8,128)} %bitcast.43, f32[]{:T(128)} %copy.54), dimensions={0}, to_apply=%region_2.3 | reduce | flops 5898240 | bytes 26738692 | tf_op jit(solution)/shard_map/reduce_sum | solution.py:88
  234.3 0.5 copy.34
  234.8 0.2 multiply_reduce_fusion
  235.0 0.5 multiply_reduce_fusion.1
  235.5 0.6 multiply_bitcast_fusion
  236.1 0.3 reduce-window.9
  236.4 0.1 slice.34
  236.5 0.1 slice_reduce_fusion
  236.6 0.1 add_bitcast_fusion
  236.7 0.7 slice_dynamic-update-slice_fusion
  237.4 11.9 %all-reduce.1 = f32[8]{0:T(128)S(1)} all-reduce(f32[8]{0:T(128)S(1)} %slice_dynamic-update-slice_fusion), channel_id=1, replica_groups=mesh['atom'=16,'mode'=8] {'mode'}, use_global_device_ids=true, to_apply=%add.1 | all-reduce | flops 8 | bytes 64
  249.3 9.7 %while.10 = (s32[]{:T(128)}, f32[]{:T(128)}, s32[]{:T(128)}, f32[8]{0:T(128)S(1)}, s32[]{:T(128)}, /*index=5*/s32[]{:T(128)}, s32[]{:T(128)}) while((s32[]{:T(128)}, f32[]{:T(128)}, s32[]{:T(128)}, f32[8]{0:T(128)S(1)}, s32[]{:T(128)}, /*index=5*/s32[]{:T(128)}, s32[]{:T(128)}) %tuple.27), condition=%wide.region_8.9_spmd, body=%wide.region_7.8_spmd.sunk | while | flops 6 | bytes 143 | solution.py:35
  249.3 0.7 dynamic_slice.10
  250.6 0.7 dynamic_slice.10
  252.0 0.7 dynamic_slice.10
  253.4 0.7 dynamic_slice.10
  254.8 0.7 dynamic_slice.10
  256.2 0.7 dynamic_slice.10
  257.6 0.7 dynamic_slice.10
  258.9 0.6 add_multiply_fusion
  (24 shorter events, 0.1 us)
Async XLA Ops:
  7.2 6.7 %copy-start = (bf16[3,256,256]{2,1,0:T(8,128)(2,1)S(1)}, bf16[3,256,256]{2,1,0:T(8,128)(2,1)}, u32[]{:S(2)}) copy-start(bf16[3,256,256]{2,1,0:T(8,128)(2,1)} %param.8) | copy-start | bytes 1179652
  7.2 12.4 %copy-start.3 = (s32[16,256]{1,0:T(8,128)S(1)}, s32[16,256]{1,0:T(8,128)}, u32[]{:S(2)}) copy-start(s32[16,256]{1,0:T(8,128)} %param.11) | copy-start | bytes 49156
  7.2 12.4 %copy-start.2 = (f32[3,3,16,256]{3,2,1,0:T(8,128)S(1)}, f32[3,3,16,256]{3,2,1,0:T(8,128)}, u32[]{:S(2)}) copy-start(f32[3,3,16,256]{3,2,1,0:T(8,128)} %param.9) | copy-start | bytes 442372
  7.2 217.8 %all-gather.4.cloned.1.call-start = ((), (), s32[]{:S(2)}) async-start(), calls=%async_computation | async-start | bytes 26738688 | tf_op jit(solution)/shard_map/all_gather | solution.py:88
  8.6 11.7 %copy-start.4 = (f32[3,16,256]{2,1,0:T(8,128)S(1)}, f32[3,16,256]{2,1,0:T(8,128)}, u32[]{:S(2)}) copy-start(f32[3,16,256]{2,1,0:T(8,128)} %param.10) | copy-start | bytes 147460
  8.8 13.3 %collective-permute-start.1 = (bf16[3,128,256]{2,0,1:T(4,128)(2,1)S(1)}, bf16[3,128,256]{2,0,1:T(4,128)(2,1)}, u32[]{:S(2)}, u32[]{:S(2)}) collective-permute-start(bf16[3,128,256]{2,0,1:T(4,128)(2,1)S(1)} %get-tuple-element.39), channel_id=1, source_target_pairs={{8,0},{16,8},{24,16},{32,24},{40,32},{48,40},{56,48},{64,56},{72,6... | collective-permute-start | bytes 589832 | tf_op jit(solution)/shard_map/ppermute | solution.py:22
  13.8 10.3 %collective-permute-start = (bf16[3,128,256]{2,0,1:T(4,128)(2,1)S(1)}, bf16[3,128,256]{2,0,1:T(4,128)(2,1)}, u32[]{:S(2)}, u32[]{:S(2)}) collective-permute-start(bf16[3,128,256]{2,0,1:T(4,128)(2,1)S(1)} %get-tuple-element.38), channel_id=1, source_target_pairs={{0,8},{8,16},{16,24},{24,32},{32,40},{40,48},{48,56},{56,64},{64,7... | collective-permute-start | bytes 589832 | tf_op jit(solution)/shard_map/ppermute | solution.py:21
  14.7 53.2 %collective-permute-start.3 = (bf16[3,256,128]{2,1,0:T(8,128)(2,1)}, bf16[3,256,128]{2,1,0:T(8,128)(2,1)}, u32[]{:S(2)}, u32[]{:S(2)}) collective-permute-start(bf16[3,256,128]{2,1,0:T(8,128)(2,1)} %get-tuple-element.41), channel_id=1, source_target_pairs={{1,0},{2,1},{3,2},{4,3},{5,4},{6,5},{7,6},{9,8},{10,9},{11,10},{12... | collective-permute-start | bytes 589832 | tf_op jit(solution)/shard_map/ppermute | solution.py:22
  18.2 49.7 %collective-permute-start.2 = (bf16[3,256,128]{2,1,0:T(8,128)(2,1)}, bf16[3,256,128]{2,1,0:T(8,128)(2,1)}, u32[]{:S(2)}, u32[]{:S(2)}) collective-permute-start(bf16[3,256,128]{2,1,0:T(8,128)(2,1)} %get-tuple-element.40), channel_id=1, source_target_pairs={{0,1},{1,2},{2,3},{3,4},{4,5},{5,6},{6,7},{8,9},{9,10},{10,11},{11... | collective-permute-start | bytes 589832 | tf_op jit(solution)/shard_map/ppermute | solution.py:21
  25.9 32.8 %copy-start.1 = (f32[3,16,256]{1,0,2:T(4,128)S(1)}, f32[3,16,256]{1,0,2:T(4,128)}, u32[]{:S(2)}) copy-start(f32[3,16,256]{1,0,2:T(4,128)} %copy.26) | copy-start | bytes 147460
  71.5 0.7 copy-start.5
  71.5 11.3 %copy-start.7 = (u32[128]{0:T(128)S(1)}, u32[128]{0:T(128)}, u32[]{:S(2)}) copy-start(u32[128]{0:T(128)} %constant.93) | copy-start | bytes 1540
  71.5 12.0 %copy-start.6 = (s32[2,256]{1,0:T(2,128)S(1)}, s32[2,256]{1,0:T(2,128)}, u32[]{:S(2)}) copy-start(s32[2,256]{1,0:T(2,128)} %param.12) | copy-start | bytes 6148
Sparse Core Ops, SparseCore 0:
  71.7 153.2 all-gather.3
